TPU v7x, 128 devices: a whole 4x4x4 slice. The times are simulated.
128 devices in a mesh: fsdp: 32 (over x, z, y_lo), tensor: 4 (over y_hi, core).
Axes of the slice: x: 4, y: 4 (y_hi: 2, y_lo: 2; y = y_hi * 2 + y_lo), z: 4, core: 2. Of those that a mesh axis runs over, the one named last changes fastest.
Arguments:
- hidden_in: bfloat16 [16384, 5120], P('fsdp', 'tensor'), may hold values from -80 to 80
- norm_gain: bfloat16 [5120], replicated, may hold values from 0.099609375 to 1.8984375
- query_weight: bfloat16 [5120, 5120], P(('fsdp', 'tensor')), may hold values from -0.078125 to 0.078125
- key_weight: bfloat16 [5120, 1024], P(('fsdp', 'tensor')), may hold values from -0.078125 to 0.078125
- value_weight: bfloat16 [5120, 1024], P(('fsdp', 'tensor')), may hold values from -0.078125 to 0.078125
- out_weight: bfloat16 [5120, 5120], P(('fsdp', 'tensor')), may hold values from -0.078125 to 0.078125
- query_bias: bfloat16 [5120], P('tensor'), may hold values from -10.5 to 10.5
- key_bias: bfloat16 [1024], P('tensor'), may hold values from -5.5 to 5.5
- value_bias: bfloat16 [1024], P('tensor'), may hold values from -3 to 3
- span_start: int32 [64], P('fsdp'), may hold values from 0 to 3839
- span_length: int32 [64], P('fsdp'), may hold values from 64 to 256, as said below
Outputs:
- attention_out: bfloat16 [16384, 5120], P('fsdp', 'tensor')
- key_cache: bfloat16 [16384, 1024], P('fsdp', 'tensor')
- value_cache: bfloat16 [16384, 1024], P('fsdp', 'tensor')
Inputs may be any that keep to these rules, and one draw needn't show every extreme that they name: `span_length`: the spans of the first rollout group are all full.
All inputs are finite; a program needn't handle non-finite values.
Results may differ from a plain program's by a relative error of at most 0.0065.
The roundings to bfloat16 on the way count: a program that leaves them out, or rounds other values in their place, can miss the bound.
Values may be sent and summed in bfloat16 or wider, within the bound.
No kernel may reach another device: no remote copies, remote signals or barrier semaphores. Data moves between devices by JAX's collectives and lax.ppermute only.
A program may use at most 128 MiB of HBM per device.

v0:
```python
import jax
import jax.numpy as jnp
from jax import lax
from jax.sharding import PartitionSpec as P

HEADS = 40
KV_HEADS = 8
HEAD = 128


rope_base = 1000000.0
epsilon = 1e-06


def rotate(entries, cosine, sine):
    half = entries.shape[-1] // 2
    first = entries[..., :half]
    second = entries[..., half:]
    return jnp.concatenate(
        [first * cosine - second * sine, second * cosine + first * sine], axis=-1
    )


def angles(span_start, span_size):
    positions = span_start[:, None] + jnp.arange(span_size, dtype=jnp.int32)[None, :]
    inverse = 1.0 / rope_base ** (jnp.arange(0, HEAD, 2, dtype=jnp.float32) / HEAD)
    phase = positions.reshape(-1).astype(jnp.float32)[:, None] * inverse[None, :]
    return (jnp.cos(phase)[:, None, :], jnp.sin(phase)[:, None, :])


def local(
    hidden_in,
    norm_gain,
    query_weight,
    key_weight,
    value_weight,
    out_weight,
    query_bias,
    key_bias,
    value_bias,
    span_start,
    span_length,
):
    slices = lax.axis_size("tensor")
    members = lax.axis_size("fsdp")
    token_rows = hidden_in.shape[0]
    local_spans = span_start.shape[0]
    span_size = token_rows // local_spans
    query_cols = query_weight.shape[1] // slices
    key_cols = key_weight.shape[1] // slices
    learner_rows = query_weight.shape[0]
    gathered = lax.all_gather(hidden_in, "tensor", axis=1, tiled=True)
    source = gathered.astype(jnp.float32)
    inverse_rms = lax.rsqrt(jnp.mean(source * source, axis=-1, keepdims=True) + epsilon)
    normed = (source * inverse_rms * norm_gain.astype(jnp.float32)).astype(jnp.bfloat16)
    joined = jnp.concatenate(
        [
            query_weight.reshape(learner_rows, slices, query_cols),
            key_weight.reshape(learner_rows, slices, key_cols),
            value_weight.reshape(learner_rows, slices, key_cols),
        ],
        axis=2,
    )
    joined_cols = joined.shape[2]
    tiled = jnp.broadcast_to(
        jnp.transpose(joined, (1, 0, 2))[None], (members, slices, learner_rows, joined_cols)
    )
    tiled = tiled.reshape(members * slices, learner_rows, joined_cols)
    arrived = lax.all_to_all(tiled, ("fsdp", "tensor"), split_axis=0, concat_axis=0, tiled=True)
    projected = jnp.dot(
        normed, arrived.reshape(-1, joined_cols), preferred_element_type=jnp.float32
    )
    query = projected[:, :query_cols] + query_bias.astype(jnp.float32)
    keys = projected[:, query_cols : query_cols + key_cols] + key_bias.astype(jnp.float32)
    values = projected[:, query_cols + key_cols :] + value_bias.astype(jnp.float32)
    local_heads = query_cols // HEAD
    local_kv = key_cols // HEAD
    groups = HEADS // KV_HEADS
    cosine, sine = angles(span_start, span_size)
    query = rotate(query.reshape(token_rows, local_heads, HEAD), cosine, sine).astype(jnp.bfloat16)
    keys = rotate(keys.reshape(token_rows, local_kv, HEAD), cosine, sine)
    live = (jnp.arange(span_size, dtype=jnp.int32)[None, :] < span_length[:, None]).reshape(
        token_rows, 1, 1
    )
    key_cache = jnp.where(live, keys, 0.0).astype(jnp.bfloat16)
    value_cache = jnp.where(live, values.reshape(token_rows, local_kv, HEAD), 0.0).astype(
        jnp.bfloat16
    )
    query_blocks = query.reshape(local_spans, span_size, local_kv, groups, HEAD)
    key_blocks = key_cache.reshape(local_spans, span_size, local_kv, HEAD)
    value_blocks = value_cache.reshape(local_spans, span_size, local_kv, HEAD)
    scores = jnp.einsum(
        "sqkgd,stkd->skgqt", query_blocks, key_blocks, preferred_element_type=jnp.float32
    ) * HEAD ** (-0.5)
    rows = jnp.arange(span_size, dtype=jnp.int32)[:, None]
    columns = jnp.arange(span_size, dtype=jnp.int32)[None, :]
    allowed = (columns <= rows)[None] & (columns[None] < span_length[:, None, None])
    scores = jnp.where(allowed[:, None, None], scores, -1e30)
    highest = jnp.max(scores, axis=-1, keepdims=True)
    raised = jnp.exp(scores - highest)
    probs = (raised / jnp.sum(raised, axis=-1, keepdims=True)).astype(jnp.bfloat16)
    mixed = jnp.einsum("skgqt,stkd->sqkgd", probs, value_blocks, preferred_element_type=jnp.float32)
    attended = mixed.reshape(token_rows, local_heads * HEAD).astype(jnp.bfloat16)
    all_heads = lax.all_gather(attended, "tensor", axis=1, tiled=True)
    out_rows_local = out_weight.shape[0]
    out_cols = out_weight.shape[1] // slices
    out_block = out_weight.reshape(out_rows_local, slices, out_cols)
    tiled_out = jnp.broadcast_to(
        jnp.transpose(out_block, (1, 0, 2))[None], (members, slices, out_rows_local, out_cols)
    )
    tiled_out = tiled_out.reshape(members * slices, out_rows_local, out_cols)
    arrived_out = lax.all_to_all(
        tiled_out, ("fsdp", "tensor"), split_axis=0, concat_axis=0, tiled=True
    )
    combined = jnp.dot(
        all_heads, arrived_out.reshape(-1, out_cols), preferred_element_type=jnp.float32
    )
    attention_out = combined.astype(jnp.bfloat16)
    return (
        attention_out,
        key_cache.reshape(token_rows, local_kv * HEAD),
        value_cache.reshape(token_rows, local_kv * HEAD),
    )


def solution(mesh):
    placed = (
        P("fsdp", "tensor"),
        P(),
        P(("fsdp", "tensor"), None),
        P(("fsdp", "tensor"), None),
        P(("fsdp", "tensor"), None),
        P(("fsdp", "tensor"), None),
        P("tensor"),
        P("tensor"),
        P("tensor"),
        P("fsdp"),
        P("fsdp"),
    )
    return jax.shard_map(
        local,
        mesh=mesh,
        in_specs=placed,
        out_specs=(P("fsdp", "tensor"), P("fsdp", "tensor"), P("fsdp", "tensor")),
        check_vma=False,
    )
```

profile of v0, /device:TPU:33, one launch (start us, length us, event | category | flops | bytes accessed | tf_op | source)
XLA Modules:
  0.0 537.0 jit_solution(14483118119026626068)
XLA Ops:
  7.2 0.9 reshape.195
  8.1 0.9 reshape.194
  9.0 1.3 reshape.193
  10.3 0.2 maximum_bitcast_fusion
  10.6 0.1 copy.19
  10.7 6.5 %broadcast_in_dim.33 = bf16[32,4,40,1792]{3,2,1,0:T(8,128)(2,1)} broadcast(bf16[4,40,1792]{2,1,0:T(8,128)(2,1)S(1)} %copy.19), dimensions={1,2,3} | broadcast | bytes 18923520 | tf_op jit(solution)/shard_map/broadcast_in_dim | solution.py:65
  17.2 0.0 copy-start.4
  17.2 0.0 copy-start.5
  17.2 0.0 copy-start.6
  17.2 0.0 copy-start.8
  17.2 0.0 copy-start.9
  17.2 0.0 copy-start.2
  17.2 10.9 %all-to-all-start = ((bf16[128,40,1792]{2,1,0:T(8,128)(2,1)}), bf16[128,40,1792]{2,1,0:T(8,128)(2,1)}, u32[]{:S(2)}, u32[]{:S(2)}) async-start(bf16[128,40,1792]{2,1,0:T(8,128)(2,1)} %bitcast.46), calls=%async_computation | async-start | bytes 36700160 | tf_op jit(solution)/shard_map/all_to_all | solution.py:69
  28.1 0.0 all-gather.3.cloned.1.call-start
  28.2 0.7 all-gather.3.cloned.1.call-update
  28.9 0.0 copy-done.4
  28.9 0.0 copy-done.5
  28.9 0.0 copy-done.6
  28.9 0.1 convert_bitcast_fusion
  29.0 0.0 copy-done.7
  29.0 0.1 iota_compare_fusion.1
  29.1 0.0 copy-done.8
  29.1 0.0 copy-done.9
  29.1 0.0 copy-done.2
  29.1 0.3 reshape.201
  29.5 0.8 broadcast_and_fusion
  30.3 0.5 multiply_cosine_fusion
  30.9 253.4 %all-gather.3.cloned.1.call-done = bf16[512,5120]{1,0:T(8,128)(2,1)} async-done(((bf16[512,1280]{1,0:T(8,128)(2,1)}), bf16[512,5120]{1,0:T(8,128)(2,1)}) %all-gather.3.cloned.1.call-update) | async-done | bytes 5242896 | tf_op jit(solution)/shard_map/all_gather | solution.py:52
  284.3 3.6 fusion.1
  287.8 1.8 all-to-all-done
  289.6 6.2 %broadcast_in_dim.41 = bf16[32,4,40,1280]{3,2,1,0:T(8,128)(2,1)} broadcast(bf16[4,40,1280]{2,1,0:T(8,128)(2,1)S(1)} %copy.30), dimensions={1,2,3} | broadcast | bytes 13516800 | tf_op jit(solution)/shard_map/broadcast_in_dim | solution.py:108
  295.9 18.2 %all-to-all-start.1 = ((bf16[128,40,1280]{2,1,0:T(8,128)(2,1)}), bf16[128,40,1280]{2,1,0:T(8,128)(2,1)}, u32[]{:S(2)}, u32[]{:S(2)}) async-start(bf16[128,40,1280]{2,1,0:T(8,128)(2,1)} %bitcast.47), calls=%async_computation.1 | async-start | bytes 26214400 | tf_op jit(solution)/shard_map/all_to_all | solution.py:112
  314.1 0.2 all-gather.5.cloned.1.call-start
  314.3 14.4 %fusion.4 = f32[512,1792]{1,0:T(8,128)S(1)} fusion(bf16[5120,1792]{1,0:T(8,128)(2,1)} %bitcast.2, bf16[512,5120]{1,0:T(8,128)(2,1)} %all-gather.3.cloned.1.call-done, f32[5120]{0:T(1024)S(1)} %convert_element_type.60, f32[512]{0:T(512)S(1)} %add_rsqrt_fusion), kind=kOutput, calls=%fused_computation.6 | convolution fusion | flops 9405726720 | bytes 27285504 | tf_op jit(solution)/shard_map/dot_general | solution.py:70
  328.7 0.0 copy-start
  328.7 1.8 copy-done
  330.5 1.7 slice_add_fusion
  332.1 2.1 copy.23
  334.3 1.3 subtract_convert_fusion
  335.6 0.2 concatenate.29
  335.7 1.3 copy.25
  337.1 0.0 copy-done.1
  337.1 0.2 concatenate.28
  337.2 1.3 copy.24
  338.6 1.1 slice_add_fusion.1
  339.7 1.0 copy.40
  340.7 1.1 multiply_subtract_fusion
  341.8 0.7 concatenate.25
  342.5 0.1 copy.39
  342.7 2.0 select_convert_fusion
  344.7 0.1 reshape.198
  344.7 0.5 copy.20
  345.2 1.4 fusion.20
  346.7 0.0 copy-start.3
  346.7 1.1 fusion.15
  347.8 0.0 copy-done.3
  347.8 1.7 fusion.27
  349.5 0.6 fusion.14
  350.1 1.4 copy.29
  351.5 1.4 copy.42
  352.9 0.0 all-gather.5.cloned.1.call-update
  352.9 142.7 %all-to-all-done.1 = bf16[128,40,1280]{2,1,0:T(8,128)(2,1)} async-done(((bf16[128,40,1280]{2,1,0:T(8,128)(2,1)}), bf16[128,40,1280]{2,1,0:T(8,128)(2,1)}, u32[]{:S(2)}, u32[]{:S(2)}) %all-to-all-start.1) | async-done | bytes 13107232 | tf_op jit(solution)/shard_map/all_to_all | solution.py:112
  495.6 21.0 %all-gather.5.cloned.1.call-done = bf16[512,5120]{0,1:T(8,128)(2,1)} async-done(((bf16[512,1280]{0,1:T(8,128)(2,1)}), bf16[512,5120]{0,1:T(8,128)(2,1)}) %all-gather.5.cloned.1.call-update) | async-done | bytes 5242896 | tf_op jit(solution)/shard_map/all_gather | solution.py:104
  516.6 13.6 %convolution_convert_fusion = bf16[512,1280]{1,0:T(8,128)(2,1)} fusion(bf16[512,5120]{0,1:T(8,128)(2,1)} %all-gather.5.cloned.1.call-done, bf16[5120,1280]{1,0:T(8,128)(2,1)} %bitcast.10), kind=kOutput, calls=%fused_computation.13 | convolution fusion | flops 6711541760 | bytes 19660800 | tf_op jit(solution)/shard_map/dot_general | solution.py:115
  (14 shorter events, 0.2 us)
Async XLA Ops:
  17.2 11.7 %copy-start.4 = (bf16[5120]{0:T(1024)(128)(2,1)S(1)}, bf16[5120]{0:T(1024)(128)(2,1)}, u32[]{:S(2)}) copy-start(bf16[5120]{0:T(1024)(128)(2,1)} %param.12) | copy-start | bytes 30724
  17.2 11.7 %copy-start.5 = (bf16[1280]{0:T(1024)(128)(2,1)S(1)}, bf16[1280]{0:T(1024)(128)(2,1)}, u32[]{:S(2)}) copy-start(bf16[1280]{0:T(1024)(128)(2,1)} %param.17) | copy-start | bytes 7684
  17.2 11.8 %copy-start.6 = (s32[2]{0:T(128)S(1)}, s32[2]{0:T(128)}, u32[]{:S(2)}) copy-start(s32[2]{0:T(128)} %param.20) | copy-start | bytes 28
  17.2 11.8 %copy-start.7 = (s32[2]{0:T(128)S(1)}, s32[2]{0:T(128)}, u32[]{:S(2)}) copy-start(s32[2]{0:T(128)} %param.21) | copy-start | bytes 28
  17.2 11.9 %copy-start.8 = (bf16[256]{0:T(256)(128)(2,1)S(1)}, bf16[256]{0:T(256)(128)(2,1)}, u32[]{:S(2)}) copy-start(bf16[256]{0:T(256)(128)(2,1)} %param.19) | copy-start | bytes 1540
  17.2 11.9 %copy-start.9 = (bf16[256]{0:T(256)(128)(2,1)S(1)}, bf16[256]{0:T(256)(128)(2,1)}, u32[]{:S(2)}) copy-start(bf16[256]{0:T(256)(128)(2,1)} %param.18) | copy-start | bytes 1540
  17.2 11.9 %copy-start.2 = (bf16[40,5120]{1,0:T(8,128)(2,1)S(1)}, bf16[40,5120]{1,0:T(8,128)(2,1)}, u32[]{:S(2)}) copy-start(bf16[40,5120]{1,0:T(8,128)(2,1)} %param.16) | copy-start | bytes 1228804
  17.2 272.4 %all-to-all-start = ((bf16[128,40,1792]{2,1,0:T(8,128)(2,1)}), bf16[128,40,1792]{2,1,0:T(8,128)(2,1)}, u32[]{:S(2)}, u32[]{:S(2)}) async-start(bf16[128,40,1792]{2,1,0:T(8,128)(2,1)} %bitcast.46), calls=%async_computation | async-start | bytes 36700160 | tf_op jit(solution)/shard_map/all_to_all | solution.py:69
  28.1 256.1 %all-gather.3.cloned.1.call-start = ((), (), s32[]{:S(2)}) async-start(), calls=%async_computation.2 | async-start | bytes 6553600 | tf_op jit(solution)/shard_map/all_gather | solution.py:52
  295.9 199.7 %all-to-all-start.1 = ((bf16[128,40,1280]{2,1,0:T(8,128)(2,1)}), bf16[128,40,1280]{2,1,0:T(8,128)(2,1)}, u32[]{:S(2)}, u32[]{:S(2)}) async-start(bf16[128,40,1280]{2,1,0:T(8,128)(2,1)} %bitcast.47), calls=%async_computation.1 | async-start | bytes 26214400 | tf_op jit(solution)/shard_map/all_to_all | solution.py:112
  314.1 202.6 %all-gather.5.cloned.1.call-start = ((), (), s32[]{:S(2)}) async-start(), calls=%async_computation.3 | async-start | bytes 6553600 | tf_op jit(solution)/shard_map/all_gather | solution.py:104
  328.7 1.8 copy-start
  335.6 1.5 copy-start.1
  346.7 1.2 copy-start.3
Sparse Core Ops, SparseCore 0:
  30.6 253.5 all-gather.2
  353.0 163.5 all-gather.4
where the time goes:
time: 538 us; the launch traced here: 537 us
  waiting for transfers between devices  420 us (78%)
  matrix products  29.7 us (6%)
  starting transfers between devices  29.4 us (5%)
  local copies, waits for them, and re-layouts  28.4 us (5%)
  other arithmetic  15.6 us (3%)
  between operations  14.3 us (3%)
    all_gather x1, waiting for transfers between devices, local(): gathered = lax.all_gather(hidden_in, 'tensor', axis=1, tiled=True)  253 us
    all_to_all x1, waiting for transfers between devices, local(): lax.all_to_all(tiled_out, ('fsdp', 'tensor'), split_axis=0, concat_axis=0...  143 us
    all_gather x1, waiting for transfers between devices, local(): all_heads = lax.all_gather(attended, 'tensor', axis=1, tiled=True)  21 us
    all_to_all x1, starting transfers between devices, local(): lax.all_to_all(tiled_out, ('fsdp', 'tensor'), split_axis=0, concat_axis=0...  18.2 us
    dot_general x1, matrix products, local(): jnp.dot(normed, arrived.reshape(-1, joined_cols), preferred_element_type=...  14.4 us
    dot_general x1, matrix products, local(): jnp.dot(all_heads, arrived_out.reshape(-1, out_cols), preferred_element_t...  13.6 us
    all_to_all x1, starting transfers between devices, local(): lax.all_to_all(tiled, ('fsdp', 'tensor'), split_axis=0, concat_axis=0, ti...  10.9 us
  transfers between devices with their start and end apart: 4, of which 4 were waited for; matrix products, arithmetic and copies ran while one was open for 8% of the time, Pallas kernels for 0%

commit v1 on v0

--- a/solution.py
+++ b/solution.py
@@ -62,11 +62,10 @@
         axis=2,
     )
     joined_cols = joined.shape[2]
-    tiled = jnp.broadcast_to(
-        jnp.transpose(joined, (1, 0, 2))[None], (members, slices, learner_rows, joined_cols)
+    exchanged = lax.all_to_all(joined, "tensor", split_axis=1, concat_axis=0, tiled=True)
+    arrived = lax.all_gather(
+        exchanged.reshape(slices * learner_rows, joined_cols), "fsdp", axis=0, tiled=True
     )
-    tiled = tiled.reshape(members * slices, learner_rows, joined_cols)
-    arrived = lax.all_to_all(tiled, ("fsdp", "tensor"), split_axis=0, concat_axis=0, tiled=True)
     projected = jnp.dot(
         normed, arrived.reshape(-1, joined_cols), preferred_element_type=jnp.float32
     )
@@ -105,12 +104,9 @@
     out_rows_local = out_weight.shape[0]
     out_cols = out_weight.shape[1] // slices
     out_block = out_weight.reshape(out_rows_local, slices, out_cols)
-    tiled_out = jnp.broadcast_to(
-        jnp.transpose(out_block, (1, 0, 2))[None], (members, slices, out_rows_local, out_cols)
-    )
-    tiled_out = tiled_out.reshape(members * slices, out_rows_local, out_cols)
-    arrived_out = lax.all_to_all(
-        tiled_out, ("fsdp", "tensor"), split_axis=0, concat_axis=0, tiled=True
+    exchanged_out = lax.all_to_all(out_block, "tensor", split_axis=1, concat_axis=0, tiled=True)
+    arrived_out = lax.all_gather(
+        exchanged_out.reshape(slices * out_rows_local, out_cols), "fsdp", axis=0, tiled=True
     )
     combined = jnp.dot(
         all_heads, arrived_out.reshape(-1, out_cols), preferred_element_type=jnp.float32

time: 538 us -> 814 us (1.51)
  waiting for transfers between devices: 420 us -> 705 us
  blocking collectives: 0 us -> 32.5 us
  starting transfers between devices: 29.4 us -> 0.16 us
  local copies, waits for them, and re-layouts: 28.4 us -> 15.7 us
    all_gather x0 -> x2, waiting for transfers between devices: none -> 639 us  [the longest x1 390 us: local(): lax.all_gather(exchanged.reshape(slices * learner_rows, joined_cols), 'fs...]
    all_gather x1, waiting for transfers between devices: 253 us -> 15.3 us  [local(): gathered = lax.all_gather(hidden_in, 'tensor', axis=1, tiled=True)]
    all_to_all x2 -> x0, waiting for transfers between devices: 145 us -> none  [the longest x1 143 us: local(): lax.all_to_all(tiled_out, ('fsdp', 'tensor'), split_axis=0, concat_axis=0...]
    all_to_all x0 -> x2, blocking collectives: none -> 32.5 us  [the longest x1 17.3 us: local(): lax.all_to_all(out_block, 'tensor', split_axis=1, concat_axis=0, tiled=True)]
    all_to_all x2 -> x0, starting transfers between devices: 29.1 us -> none  [the longest x1 18.2 us: local(): lax.all_to_all(tiled_out, ('fsdp', 'tensor'), split_axis=0, concat_axis=0...]
    all_gather x1, waiting for transfers between devices: 21 us -> 49.5 us  [local(): all_heads = lax.all_gather(attended, 'tensor', axis=1, tiled=True)]
    broadcast_in_dim x2 -> x0, local copies, waits for them, and re-layouts: 12.7 us -> none  [the longest x1 6.51 us: local(): jnp.broadcast_to(jnp.transpose(joined, (1, 0, 2))[None], (members, slices...]
  transfers between devices with their start and end apart: 4 -> 4, of which waited for: 4 -> 4; matrix products, arithmetic and copies ran while one was open for 8% -> 6% of each run, Pallas kernels for 0% -> 0%
where the time goes in v1:
time: 814 us; the launch traced here: 812 us
  waiting for transfers between devices  705 us (87%)
  blocking collectives  32.5 us (4%)
  matrix products  29.6 us (4%)
  local copies, waits for them, and re-layouts  15.7 us (2%)
  other arithmetic  15.4 us (2%)
  between operations  14.1 us (2%)
    all_gather x1, waiting for transfers between devices, local(): lax.all_gather(exchanged.reshape(slices * learner_rows, joined_cols), 'fs...  390 us
    all_gather x1, waiting for transfers between devices, local(): lax.all_gather(exchanged_out.reshape(slices * out_rows_local, out_cols),...  249 us
    all_gather x1, waiting for transfers between devices, local(): all_heads = lax.all_gather(attended, 'tensor', axis=1, tiled=True)  49.5 us
    all_to_all x1, blocking collectives, local(): lax.all_to_all(out_block, 'tensor', split_axis=1, concat_axis=0, tiled=True)  17.3 us
  transfers between devices with their start and end apart: 4, of which 4 were waited for; matrix products, arithmetic and copies ran while one was open for 6% of the time, Pallas kernels for 0%

profile of v1, /device:TPU:33, one launch (start us, length us, event | category | flops | bytes accessed | tf_op | source)
XLA Modules:
  0.0 812.1 jit_solution(5852832301626456153)
XLA Ops:
  7.2 0.0 copy-start.3
  7.2 0.0 all-gather.5.cloned.1.call-start
  7.2 0.7 all-gather.5.cloned.1.call-update
  7.9 0.0 copy-start.5
  7.9 0.0 copy-start.8
  7.9 0.0 copy-start.7
  7.9 0.0 copy-start.9
  8.0 0.0 copy-start.10
  8.0 0.0 copy-start.6
  8.0 0.0 all-gather.7.cloned.1.call-start
  8.0 1.3 reshape.187
  9.3 0.9 reshape.188
  10.3 0.9 reshape.189
  11.2 0.2 pad_maximum_fusion
  11.4 0.1 copy.41
  11.5 15.2 %all_to_all.30 = bf16[40,4,1792]{2,0,1:T(8,128)(2,1)} all-to-all(bf16[40,4,1792]{2,0,1:T(8,128)(2,1)S(1)} %copy.41), channel_id=1, replica_groups=mesh['fsdp'=32,'tensor'=4] {'tensor'}, dimensions={1} | all-to-all | bytes 1146880 | tf_op jit(solution)/shard_map/all_to_all | solution.py:65
  26.7 0.0 all-gather.7.cloned.1.call-update
  26.8 0.0 all-gather.11.cloned.1.call-start
  26.8 0.0 copy-done.3
  26.9 17.3 %all_to_all.31 = bf16[40,4,1280]{2,0,1:T(8,128)(2,1)} all-to-all(bf16[40,4,1280]{2,0,1:T(8,128)(2,1)S(1)} %bitcast.59), channel_id=1, replica_groups=mesh['fsdp'=32,'tensor'=4] {'tensor'}, dimensions={1} | all-to-all | bytes 819200 | tf_op jit(solution)/shard_map/all_to_all | solution.py:107
  44.2 0.0 all-gather.11.cloned.1.call-update
  44.2 0.0 all-gather.9.cloned.1.call-start
  44.2 0.0 copy-done.5
  44.3 0.0 copy-done.8
  44.3 0.0 copy-done.7
  44.3 0.1 convert_bitcast_fusion
  44.4 0.0 copy-done.9
  44.4 0.1 iota_compare_fusion.1
  44.5 0.0 copy-done.10
  44.5 0.8 broadcast_and_fusion
  45.3 0.5 multiply_cosine_fusion
  45.9 15.3 %all-gather.5.cloned.1.call-done = bf16[512,5120]{1,0:T(8,128)(2,1)} async-done(((bf16[512,1280]{1,0:T(8,128)(2,1)}), bf16[512,5120]{1,0:T(8,128)(2,1)}) %all-gather.5.cloned.1.call-update) | async-done | bytes 5242896 | tf_op jit(solution)/shard_map/all_gather | solution.py:52
  61.2 3.6 fusion.1
  64.8 389.9 %all-gather.7.cloned.1.call-done = bf16[5120,1792]{1,0:T(8,128)(2,1)} async-done(((bf16[160,1792]{1,0:T(8,128)(2,1)}), bf16[5120,1792]{1,0:T(8,128)(2,1)}) %all-gather.7.cloned.1.call-update) | async-done | bytes 18350096 | tf_op jit(solution)/shard_map/all_gather | solution.py:66
  454.7 14.4 %fusion.4 = f32[512,1792]{1,0:T(8,128)S(1)} fusion(bf16[5120,1792]{1,0:T(8,128)(2,1)} %all-gather.7.cloned.1.call-done, bf16[512,5120]{1,0:T(8,128)(2,1)} %all-gather.5.cloned.1.call-done, f32[5120]{0:T(1024)S(1)} %convert_element_type.60, f32[512]{0:T(512)S(1)} %add_rsqrt_fusion), kind=kOutput, calls=%fused_computation.6 | convolution fusion | flops 9405726720 | bytes 27285504 | tf_op jit(solution)/shard_map/dot_general | solution.py:69
  469.1 0.0 copy-start
  469.1 1.8 copy-done
  470.9 0.2 copy.62
  471.1 0.1 multiply_subtract_fusion
  471.2 0.7 concatenate.25
  471.9 0.7 concatenate.26
  472.6 0.1 copy.61
  472.7 2.0 select_convert_fusion
  474.7 0.1 reshape.191
  474.8 1.0 copy.42
  475.8 3.4 slice_add_fusion
  479.2 2.2 copy.45
  481.4 1.3 subtract_convert_fusion
  482.6 0.2 concatenate.28
  482.8 1.3 copy.46
  484.2 0.2 concatenate.29
  484.3 1.3 copy.47
  485.7 0.0 copy-done.2
  485.7 1.5 fusion.20
  487.2 0.0 copy-start.4
  487.2 1.2 fusion.15
  488.3 1.7 fusion.27
  490.0 0.6 fusion.14
  490.6 1.4 copy.51
  492.0 1.4 copy.65
  493.3 0.0 all-gather.9.cloned.1.call-update
  493.3 249.1 %all-gather.11.cloned.1.call-done = bf16[5120,1280]{1,0:T(8,128)(2,1)} async-done(((bf16[160,1280]{1,0:T(8,128)(2,1)}), bf16[5120,1280]{1,0:T(8,128)(2,1)}) %all-gather.11.cloned.1.call-update) | async-done | bytes 13107216 | tf_op jit(solution)/shard_map/all_gather | solution.py:108
  742.4 49.5 %all-gather.9.cloned.1.call-done = bf16[512,5120]{0,1:T(8,128)(2,1)} async-done(((bf16[512,1280]{0,1:T(8,128)(2,1)}), bf16[512,5120]{0,1:T(8,128)(2,1)}) %all-gather.9.cloned.1.call-update) | async-done | bytes 5242896 | tf_op jit(solution)/shard_map/all_gather | solution.py:103
  792.0 13.6 %convolution_convert_fusion = bf16[512,1280]{1,0:T(8,128)(2,1)} fusion(bf16[512,5120]{0,1:T(8,128)(2,1)} %all-gather.9.cloned.1.call-done, bf16[5120,1280]{1,0:T(8,128)(2,1)} %all-gather.11.cloned.1.call-done), kind=kOutput, calls=%fused_computation.13 | convolution fusion | flops 6711541760 | bytes 19660800 | tf_op jit(solution)/shard_map/dot_general | solution.py:111
  (17 shorter events, 0.2 us)
Async XLA Ops:
  7.2 19.7 %copy-start.3 = (bf16[40,5120]{1,0:T(8,128)(2,1)S(1)}, bf16[40,5120]{1,0:T(8,128)(2,1)}, u32[]{:S(2)}) copy-start(bf16[40,5120]{1,0:T(8,128)(2,1)} %param.16) | copy-start | bytes 1228804
  7.2 54.0 %all-gather.5.cloned.1.call-start = ((), (), s32[]{:S(2)}) async-start(), calls=%async_computation.2 | async-start | bytes 6553600 | tf_op jit(solution)/shard_map/all_gather | solution.py:52
  7.9 36.3 %copy-start.5 = (bf16[5120]{0:T(1024)(128)(2,1)S(1)}, bf16[5120]{0:T(1024)(128)(2,1)}, u32[]{:S(2)}) copy-start(bf16[5120]{0:T(1024)(128)(2,1)} %param.12) | copy-start | bytes 30724
  7.9 36.3 %copy-start.8 = (bf16[256]{0:T(256)(128)(2,1)S(1)}, bf16[256]{0:T(256)(128)(2,1)}, u32[]{:S(2)}) copy-start(bf16[256]{0:T(256)(128)(2,1)} %param.18) | copy-start | bytes 1540
  7.9 36.4 %copy-start.7 = (s32[2]{0:T(128)S(1)}, s32[2]{0:T(128)}, u32[]{:S(2)}) copy-start(s32[2]{0:T(128)} %param.20) | copy-start | bytes 28
  7.9 36.4 %copy-start.9 = (s32[2]{0:T(128)S(1)}, s32[2]{0:T(128)}, u32[]{:S(2)}) copy-start(s32[2]{0:T(128)} %param.21) | copy-start | bytes 28
  8.0 36.5 %copy-start.10 = (bf16[256]{0:T(256)(128)(2,1)S(1)}, bf16[256]{0:T(256)(128)(2,1)}, u32[]{:S(2)}) copy-start(bf16[256]{0:T(256)(128)(2,1)} %param.19) | copy-start | bytes 1540
  8.0 36.5 %copy-start.6 = (bf16[1280]{0:T(1024)(128)(2,1)S(1)}, bf16[1280]{0:T(1024)(128)(2,1)}, u32[]{:S(2)}) copy-start(bf16[1280]{0:T(1024)(128)(2,1)} %param.17) | copy-start | bytes 7684
  8.0 446.7 %all-gather.7.cloned.1.call-start = ((), (), s32[]{:S(2)}) async-start(), calls=%async_computation.3 | async-start | bytes 18923520 | tf_op jit(solution)/shard_map/all_gather | solution.py:66
  26.8 715.7 %all-gather.11.cloned.1.call-start = ((), (), s32[]{:S(2)}) async-start(), calls=%async_computation.5 | async-start | bytes 13516800 | tf_op jit(solution)/shard_map/all_gather | solution.py:108
  44.2 747.8 %all-gather.9.cloned.1.call-start = ((), (), s32[]{:S(2)}) async-start(), calls=%async_computation.4 | async-start | bytes 6553600 | tf_op jit(solution)/shard_map/all_gather | solution.py:103
  469.1 1.8 copy-start
  482.6 1.5 copy-start.1
  482.6 3.0 copy-start.2
  487.2 1.2 copy-start.4
Sparse Core Ops, SparseCore 0:
  9.7 51.4 all-gather.4
  62.8 391.8 all-gather.6
  456.3 286.0 all-gather.10
  744.5 47.4 all-gather.8
